TPU v7x, 32 devices: a whole 2x2x4 slice. The times are simulated.
32 devices in a mesh: group: 2 (over y), tensor: 4 (over z), dp: 4 (over x, core).
Axes of the slice: x: 2, y: 2, z: 4, core: 2. Of those that a mesh axis runs over, the one named last changes fastest.
Arguments:
- teacher_input: bfloat16 [16, 257, 6144], P(('group', 'dp')), parts along dimension 0, may hold values from -1000 to 1000
- teacher_gain: float32 [6144], replicated, may hold values from 0.5 to 2
- teacher_weight: bfloat16 [6144, 2, 6144], P('dp', None, 'tensor'), may hold values from -30 to 30
- head_counts: int32 [48, 16], replicated, may hold values from 0 to 3
- assignment: int32 [16], P(('group', 'dp')), parts along dimension 0, may hold values from 0 to 7, each once
- student_input: bfloat16 [16, 257, 1024], P(('group', 'dp')), parts along dimension 0, may hold values from -1000 to 1000
- student_gain: float32 [1024], replicated, may hold values from 0.5 to 2
- student_bias: float32 [1024], replicated, may hold values from -3 to 3
- student_weight: bfloat16 [1024, 2048], P(None, 'tensor'), may hold values from -30 to 30
Outputs:
- weight_grad: float32 [2048, 2048], P('group', 'tensor'), parts along dimension 0
There are 2 independent parts, one for each index of `group`. A program takes and returns all parts, laid end to end along the dimension named above; an argument that names none is the same for every part. Nothing has to cross between parts.
Inputs may be any that keep to these rules, and one draw needn't show every extreme that they name: `assignment`: every image index of the group appears exactly once.
All inputs are finite; a program needn't handle non-finite values.
Results may differ from a plain program's by a relative error of at most 0.013.
The roundings to bfloat16 on the way count: a program that leaves them out, or rounds other values in their place, can miss the bound.
Values may be sent and summed in bfloat16 or wider, within the bound.
A program may use at most 192 MiB of HBM per device.

v0:
```python
import jax
import jax.numpy as jnp
from jax import lax
from jax.sharding import PartitionSpec as P

HD_T = 128
D_S = 1024
HD_S = 64
QROWS = 128
DIVISOR = 72


def layer_norm(values, gain, shift):
    wide = values.astype(jnp.float32)
    center = wide - jnp.mean(wide, axis=-1, keepdims=True)
    spread = jnp.mean(center * center, axis=-1, keepdims=True)
    return center * lax.rsqrt(spread + 1e-06) * gain + shift


def on_device(
    teacher_input,
    teacher_gain,
    teacher_weight,
    head_counts,
    assignment,
    student_input,
    student_gain,
    student_bias,
    student_weight,
):
    images = teacher_input.shape[0]
    tokens = teacher_input.shape[1]
    width_t = teacher_input.shape[2]
    teacher_cols = teacher_weight.shape[2]
    heads_here = teacher_cols // HD_T
    student_heads = student_weight.shape[1] // (2 * HD_S)
    tensor_place = lax.axis_index("tensor")
    teacher_normed = layer_norm(teacher_input, teacher_gain, 0.0).astype(jnp.bfloat16)
    normed_query = teacher_normed[:, :QROWS].reshape(images * QROWS, width_t)
    normed_keys = teacher_normed.reshape(images * tokens, width_t)
    piece = lax.all_gather(teacher_weight, "dp", axis=0, tiled=True)
    new_query = jnp.dot(normed_query, piece[:, 0, :], preferred_element_type=jnp.float32)
    new_keys = jnp.dot(normed_keys, piece[:, 1, :], preferred_element_type=jnp.float32)
    teacher_query = (
        (new_query * HD_T ** (-0.5)).astype(jnp.bfloat16).reshape(images, QROWS, heads_here, HD_T)
    )
    teacher_keys = new_keys.astype(jnp.bfloat16).reshape(images, tokens, heads_here, HD_T)
    teacher_scores = jnp.einsum(
        "bqhd,bkhd->bhqk", teacher_query, teacher_keys, preferred_element_type=jnp.float32
    )
    teacher_maps = jax.nn.softmax(teacher_scores, axis=-1).astype(jnp.bfloat16)
    own_counts = lax.dynamic_slice_in_dim(
        head_counts, tensor_place * heads_here, heads_here, 0
    ).astype(jnp.bfloat16)
    folded = lax.psum_scatter(
        (
            jnp.einsum(
                "bgqk,gs->sbqk", teacher_maps, own_counts, preferred_element_type=jnp.float32
            )
            / DIVISOR
        ).astype(jnp.bfloat16),
        "tensor",
        scatter_dimension=0,
        tiled=True,
    )
    piece = lax.all_gather(folded, "dp", axis=1, tiled=True)
    width_piece = piece.shape[1]
    positions = jnp.arange(width_piece, dtype=jnp.int32)
    picker = (assignment[:, None] == positions[None, :]).astype(jnp.bfloat16)
    target = jnp.einsum("ji,hiqk->hjqk", picker, piece, preferred_element_type=jnp.float32).astype(
        jnp.bfloat16
    )
    student_normed = layer_norm(student_input, student_gain, student_bias).astype(jnp.bfloat16)
    normed_front = student_normed[:, :QROWS]
    packed = student_weight.reshape(D_S, student_heads, 2, HD_S)
    weight_query = packed[:, :, 0, :].reshape(D_S, student_heads * HD_S)
    weight_key = packed[:, :, 1, :].reshape(D_S, student_heads * HD_S)
    student_query = (
        jnp.einsum("btd,dc->btc", normed_front, weight_query, preferred_element_type=jnp.float32)
        * HD_S ** (-0.5)
    ).astype(jnp.bfloat16)
    student_keys = jnp.einsum(
        "btd,dc->btc", student_normed, weight_key, preferred_element_type=jnp.float32
    ).astype(jnp.bfloat16)
    split_query = student_query.reshape(images, QROWS, student_heads, HD_S)
    split_keys = student_keys.reshape(images, tokens, student_heads, HD_S)
    probs = jax.nn.softmax(
        jnp.einsum("bqhd,bkhd->hbqk", split_query, split_keys, preferred_element_type=jnp.float32),
        axis=-1,
    )
    target_wide = target.astype(jnp.float32)
    score_grad = (probs * jnp.sum(target_wide, axis=-1, keepdims=True) - target_wide).astype(
        jnp.bfloat16
    )
    query_grad = (
        jnp.einsum("hbqk,bkhd->bqhd", score_grad, split_keys, preferred_element_type=jnp.float32)
        * HD_S ** (-0.5)
    ).astype(jnp.bfloat16)
    key_grad = jnp.einsum(
        "hbqk,bqhd->bkhd", score_grad, split_query, preferred_element_type=jnp.float32
    ).astype(jnp.bfloat16)
    grad_query = jnp.einsum(
        "fkm,fkp->mp",
        normed_front,
        query_grad.reshape(images, QROWS, student_heads * HD_S),
        preferred_element_type=jnp.float32,
    )
    grad_key = jnp.einsum(
        "oip,ois->ps",
        student_normed,
        key_grad.reshape(images, tokens, student_heads * HD_S),
        preferred_element_type=jnp.float32,
    )
    local_grad = jnp.stack(
        [grad_query.reshape(D_S, student_heads, HD_S), grad_key.reshape(D_S, student_heads, HD_S)],
        axis=2,
    )
    local_grad = local_grad.reshape(D_S, student_heads * 2 * HD_S)
    return lax.psum(local_grad.astype(jnp.bfloat16), "dp").astype(jnp.float32)


def solution(mesh):
    placed = (
        P(("group", "dp"), None, None),
        P(),
        P("dp", None, "tensor"),
        P(),
        P(("group", "dp")),
        P(("group", "dp"), None, None),
        P(),
        P(),
        P(None, "tensor"),
    )
    return jax.shard_map(
        on_device, mesh=mesh, in_specs=placed, out_specs=P("group", "tensor"), check_vma=False
    )
```

profile of v0, /device:TPU:0, one launch (start us, length us, event | category | flops | bytes accessed | tf_op | source)
XLA Modules:
  0.0 448.8 jit_solution(8952922629155033750)
XLA Ops:
  6.5 8.8 %copy.104 = bf16[1536,2,1536]{2,0,1:T(8,128)(2,1)} copy(bf16[1536,2,1536]{2,1,0:T(2,128)(2,1)} %param.11) | data formatting | bytes 18874368 | tf_op args[2]
  15.4 6.3 %convert_reduce_fusion = f32[2,257]{1,0:T(2,128)S(1)} fusion(bf16[2,257,6144]{2,0,1:T(2,128)(2,1)} %param.9), kind=kLoop, calls=%fused_computation.6 | loop fusion | flops 6315518 | bytes 6318088 | tf_op jit(solution)/shard_map/reduce_sum | solution.py:15
  21.7 3.5 fusion.5
  25.2 4.1 fusion.7
  29.4 4.6 %copy-done.1 = bf16[2,257,6144]{2,1,0:T(8,128)(2,1)} copy-done((bf16[2,257,6144]{2,1,0:T(8,128)(2,1)}, bf16[2,257,6144]{2,1,0:T(8,128)(2,1)S(1)}, u32[]{:S(2)}) %copy-start.1) | copy-done | bytes 6316056
  34.0 9.8 %reshape.81 = bf16[514,6144]{1,0:T(8,128)(2,1)} reshape(bf16[2,257,6144]{2,1,0:T(8,128)(2,1)} %copy-done.1) | data formatting | bytes 12632064 | tf_op jit(solution)/shard_map/reshape | solution.py:40
  43.7 202.4 %all-gather.3.cloned.1.call-done = bf16[6144,2,1536]{2,0,1:T(8,128)(2,1)} async-done(((bf16[1536,2,1536]{2,0,1:T(8,128)(2,1)}), bf16[6144,2,1536]{2,0,1:T(8,128)(2,1)}) %all-gather.3.cloned.1.call-update) | async-done | bytes 37748752 | tf_op jit(solution)/shard_map/all_gather | solution.py:41
  246.1 10.2 %fusion.10 = bf16[256,1536]{1,0:T(8,128)(2,1)} fusion(bf16[256,6144]{1,0:T(8,128)(2,1)S(1)} %bitcast.99, bf16[6144,2,1536]{2,0,1:T(8,128)(2,1)} %all-gather.3.cloned.1.call-done), kind=kOutput, calls=%fused_computation.19 | convolution fusion | flops 4832624640 | bytes 22806528 | tf_op jit(solution)/shard_map/dot_general | solution.py:42
  256.3 2.4 reshape.95
  258.6 16.2 %fusion.8 = bf16[514,1536]{1,0:T(8,128)(2,1)S(1)} fusion(bf16[514,6144]{1,0:T(8,128)(2,1)} %reshape.81, bf16[6144,2,1536]{2,0,1:T(8,128)(2,1)} %all-gather.3.cloned.1.call-done), kind=kOutput, calls=%fused_computation.15 | convolution fusion | flops 9702214656 | bytes 26843136 | tf_op jit(solution)/shard_map/dot_general | solution.py:43
  274.8 2.4 reshape.82
  277.2 3.1 fusion.61
  281.1 0.8 multiply_convert_fusion
  281.8 2.9 copy.109
  284.9 0.6 dynamic-slice
  286.1 85.7 %all-reduce.6.cloned.1.call-done = bf16[16,2,128,257]{2,1,3,0:T(2,128)(2,1)} async-done(((bf16[16,2,128,257]{2,1,3,0:T(2,128)(2,1)}), bf16[16,2,128,257]{2,1,3,0:T(2,128)(2,1)}) %all-reduce.6.cloned.1.call-update) | async-done | bytes 2105360
  371.8 1.4 constant_dynamic-slice_fusion
  373.2 1.0 copy.110
  374.3 0.8 copy.94
  376.1 0.8 convolution_convert_fusion.1
  377.1 0.5 fusion.16
  377.6 1.0 copy-done.3
  379.0 0.5 fusion.66
  379.6 0.5 fusion.34
  380.1 16.0 %all-gather.5.cloned.1.call-done = bf16[4,8,128,257]{2,0,3,1:T(4,128)(2,1)} async-done(((bf16[4,2,128,257]{2,0,3,1:T(4,128)(2,1)}), bf16[4,8,128,257]{2,0,3,1:T(4,128)(2,1)}) %all-gather.5.cloned.1.call-update) | async-done | bytes 2105360 | tf_op jit(solution)/shard_map/all_gather | solution.py:66
  396.1 2.4 fusion.17
  398.8 0.7 fusion.31
  399.4 1.5 fusion.24
  401.0 1.0 fusion.25
  402.1 1.1 copy.117
  403.2 36.5 %all-reduce.4.cloned.1.call-done = bf16[1024,512]{0,1:T(8,128)(2,1)} async-done(((bf16[1024,512]{0,1:T(8,128)(2,1)}), bf16[1024,512]{0,1:T(8,128)(2,1)}) %all-reduce.4.cloned.1.call-update) | async-done | bytes 1048592 | tf_op jit(solution)/shard_map/psum | solution.py:119
  439.7 2.6 copy.118
  (44 shorter events, 3.0 us)
Async XLA Ops:
  6.5 239.5 %all-gather.3.cloned.1.call-start = ((), (), s32[]{:S(2)}) async-start(), calls=%async_computation | async-start | bytes 47185920 | tf_op jit(solution)/shard_map/all_gather | solution.py:41
  15.3 356.5 %all-reduce.6.cloned.1.call-start = ((), (), s32[]{:S(2)}) async-start(), calls=%async_computation.3 | async-start | bytes 4210688
  15.4 6.3 %copy-start = (bf16[2,257,6144]{2,0,1:T(2,128)(2,1)S(1)}, bf16[2,257,6144]{2,0,1:T(2,128)(2,1)}, u32[]{:S(2)}) copy-start(bf16[2,257,6144]{2,0,1:T(2,128)(2,1)} %param.9) | copy-start | bytes 18948100
  21.7 3.5 copy-start.5
  29.4 4.6 %copy-start.1 = (bf16[2,257,6144]{2,1,0:T(8,128)(2,1)}, bf16[2,257,6144]{2,1,0:T(8,128)(2,1)S(1)}, u32[]{:S(2)}) copy-start(bf16[2,257,6144]{2,1,0:T(8,128)(2,1)S(1)} %fusion.7) | copy-start | bytes 18948100
  34.0 212.1 %slice-start = ((bf16[2,257,6144]{2,1,0:T(8,128)(2,1)}), bf16[2,128,6144]{2,1,0:T(8,128)(2,1)S(1)}, s32[]{:S(2)}) async-start(bf16[2,257,6144]{2,1,0:T(8,128)(2,1)} %copy-done.1), calls=%async_computation.4 | async-start | bytes 6291456 | tf_op jit(solution)/shard_map/slice | solution.py:39
  280.4 0.7 copy-start.6
  281.8 3.0 copy-start.10
  284.8 89.5 %copy-start.4 = (bf16[1024,512]{1,0:T(8,128)(2,1)S(1)}, bf16[1024,512]{1,0:T(8,128)(2,1)}, u32[]{:S(2)}) copy-start(bf16[1024,512]{1,0:T(8,128)(2,1)} %param.17) | copy-start | bytes 3145732
  284.8 111.3 %all-gather.5.cloned.1.call-start = ((), (), s32[]{:S(2)}) async-start(), calls=%async_computation.1 | async-start | bytes 2631680 | tf_op jit(solution)/shard_map/all_gather | solution.py:66
  286.1 89.0 %copy-start.2 = (bf16[2,257,1024]{2,0,1:T(2,128)(2,1)S(1)}, bf16[2,257,1024]{2,0,1:T(2,128)(2,1)}, u32[]{:S(2)}) copy-start(bf16[2,257,1024]{2,0,1:T(2,128)(2,1)} %param.14) | copy-start | bytes 3158020
  374.3 65.4 %all-reduce.4.cloned.1.call-start = ((), (), s32[]{:S(2)}) async-start(), calls=%async_computation.2 | async-start | bytes 2097152 | tf_op jit(solution)/shard_map/psum | solution.py:119
  375.1 0.9 copy-start.7
  375.1 0.9 copy-start.8
  377.6 1.0 copy-start.3
  378.6 17.5 %copy-start.9 = (s32[2]{0:T(128)S(1)}, s32[2]{0:T(128)}, u32[]{:S(2)}) copy-start(s32[2]{0:T(128)} %param.13) | copy-start | bytes 28
Sparse Core Ops, SparseCore 0:
  15.5 230.5 all-gather.2
  284.9 86.8 all-reduce.5
  374.4 21.6 all-gather.4
  403.3 36.2 all-reduce.3
where the time goes:
time: 449 us
  waiting for transfers between devices  341 us (76%)
  local copies, waits for them, and re-layouts  40.2 us (9%)
  matrix products  36.8 us (8%)
  other arithmetic  17.1 us (4%)
  between operations  14 us (3%)
    all_gather x1, waiting for transfers between devices, on_device(): piece = lax.all_gather(teacher_weight, 'dp', axis=0, tiled=True)  202 us
    unnamed x5, waiting for transfers between devices  85.8 us
    psum x1, waiting for transfers between devices, on_device(): return lax.psum(local_grad.astype(jnp.bfloat16), 'dp').astype(jnp.float32)  36.5 us
    unnamed x26, local copies, waits for them, and re-layouts  17.6 us
    dot_general x1, matrix products, on_device(): jnp.dot(normed_keys, piece[:, 1, :], preferred_element_type=jnp.float32)  16.2 us
    all_gather x1, waiting for transfers between devices, on_device(): piece = lax.all_gather(folded, 'dp', axis=1, tiled=True)  16 us
    dot_general x1, matrix products, on_device(): jnp.dot(normed_query, piece[:, 0, :], preferred_element_type=jnp.float32)  10.2 us
    reshape x1, local copies, waits for them, and re-layouts, on_device(): normed_keys = teacher_normed.reshape(images * tokens, width_t)  9.77 us
  transfers between devices with their start and end apart: 4, of which 4 were waited for; matrix products, arithmetic and copies ran while one was open for 6% of the time, Pallas kernels for 0%

commit v1 on v0

--- a/solution.py
+++ b/solution.py
@@ -38,7 +38,12 @@
     teacher_normed = layer_norm(teacher_input, teacher_gain, 0.0).astype(jnp.bfloat16)
     normed_query = teacher_normed[:, :QROWS].reshape(images * QROWS, width_t)
     normed_keys = teacher_normed.reshape(images * tokens, width_t)
-    piece = lax.all_gather(teacher_weight, "dp", axis=0, tiled=True)
+    ring = [teacher_weight]
+    for hop in range(3):
+        ring.append(lax.ppermute(ring[-1], "dp", [(dev, (dev + 1) % 4) for dev in range(4)]))
+    piece = jnp.roll(
+        jnp.concatenate(ring[::-1], axis=0), (lax.axis_index("dp") + 1) * ring[0].shape[0], axis=0
+    )
     new_query = jnp.dot(normed_query, piece[:, 0, :], preferred_element_type=jnp.float32)
     new_keys = jnp.dot(normed_keys, piece[:, 1, :], preferred_element_type=jnp.float32)
     teacher_query = (

time: 449 us -> 610 us (1.36); the launches traced: 449 us -> 603 us
  waiting for transfers between devices: 341 us -> 430 us
  local copies, waits for them, and re-layouts: 40.2 us -> 104 us
    ppermute x0 -> x3, waiting for transfers between devices: none -> 289 us  [on_device(): lax.ppermute(ring[-1], 'dp', [(dev, (dev + 1) % 4) for dev in range(4)])]
    all_gather x1 -> x0, waiting for transfers between devices: 202 us -> none  [on_device(): piece = lax.all_gather(teacher_weight, 'dp', axis=0, tiled=True)]
    unnamed x26 -> x35, local copies, waits for them, and re-layouts: 17.6 us -> 75.4 us
    concatenate x0 -> x1, local copies, waits for them, and re-layouts: none -> 8.82 us  [on_device(): jnp.roll(jnp.concatenate(ring[::-1], axis=0), (lax.axis_index('dp') + 1)...]
    unnamed x5 -> x4, waiting for transfers between devices: 85.8 us -> 88 us
  transfers between devices with their start and end apart: 4 -> 6, of which waited for: 4 -> 6; matrix products, arithmetic and copies ran while one was open for 6% -> 4% of each run, Pallas kernels for 0% -> 0%
where the time goes in v1:
time: 610 us; the launch traced here: 603 us
  waiting for transfers between devices  430 us (70%)
  local copies, waits for them, and re-layouts  104 us (17%)
  matrix products  37 us (6%)
  other arithmetic  17.2 us (3%)
  between operations  14.3 us (2%)
    ppermute x3, waiting for transfers between devices, on_device(): lax.ppermute(ring[-1], 'dp', [(dev, (dev + 1) % 4) for dev in range(4)])  289 us
    unnamed x4, waiting for transfers between devices  88 us
    unnamed x35, local copies, waits for them, and re-layouts  75.4 us
    psum x1, waiting for transfers between devices, on_device(): return lax.psum(local_grad.astype(jnp.bfloat16), 'dp').astype(jnp.float32)  36.5 us
    all_gather x1, waiting for transfers between devices, on_device(): piece = lax.all_gather(folded, 'dp', axis=1, tiled=True)  16 us
    dot_general x1, matrix products, on_device(): jnp.dot(normed_keys, piece[:, 1, :], preferred_element_type=jnp.float32)  16 us
  transfers between devices with their start and end apart: 6, of which 6 were waited for; matrix products, arithmetic and copies ran while one was open for 4% of the time, Pallas kernels for 0%

profile of v1, /device:TPU:0, one launch (start us, length us, event | category | flops | bytes accessed | tf_op | source)
XLA Modules:
  0.0 602.8 jit_solution(256224490272378922)
XLA Ops:
  6.5 8.8 %copy.110 = bf16[1536,2,1536]{2,0,1:T(8,128)(2,1)} copy(bf16[1536,2,1536]{2,1,0:T(2,128)(2,1)} %param.11) | data formatting | bytes 18874368 | tf_op args[2]
  15.8 104.5 %collective-permute-done = bf16[1536,2,1536]{2,0,1:T(8,128)(2,1)S(1)} collective-permute-done((bf16[1536,2,1536]{2,0,1:T(8,128)(2,1)}, bf16[1536,2,1536]{2,0,1:T(8,128)(2,1)S(1)}, u32[]{:S(2)}, u32[]{:S(2)}) %collective-permute-start) | collective-permute-done | bytes 9437216 | tf_op jit(solution)/shard_map/ppermute | solution.py:43
  120.3 3.7 copy-done.2
  124.0 104.2 %collective-permute-done.1 = bf16[1536,2,1536]{2,0,1:T(8,128)(2,1)} collective-permute-done((bf16[1536,2,1536]{2,0,1:T(8,128)(2,1)S(1)}, bf16[1536,2,1536]{2,0,1:T(8,128)(2,1)}, u32[]{:S(2)}, u32[]{:S(2)}) %collective-permute-start.1) | collective-permute-done | bytes 9437216 | tf_op jit(solution)/shard_map/ppermute | solution.py:43
  228.2 6.3 %convert_reduce_fusion = f32[2,257]{1,0:T(2,128)S(1)} fusion(bf16[2,257,6144]{2,0,1:T(2,128)(2,1)} %param.9), kind=kLoop, calls=%fused_computation.6 | loop fusion | flops 6315518 | bytes 6318088 | tf_op jit(solution)/shard_map/reduce_sum | solution.py:15
  234.5 3.5 fusion.5
  238.0 4.2 fusion.7
  242.3 2.7 copy-done.1
  245.0 6.9 %reshape.81 = bf16[514,6144]{1,0:T(8,128)(2,1)} reshape(bf16[2,257,6144]{2,1,0:T(8,128)(2,1)} %copy-done.1) | data formatting | bytes 12632064 | tf_op jit(solution)/shard_map/reshape | solution.py:40
  251.9 80.7 %collective-permute-done.2 = bf16[1536,2,1536]{2,0,1:T(8,128)(2,1)} collective-permute-done((bf16[1536,2,1536]{2,0,1:T(8,128)(2,1)}, bf16[1536,2,1536]{2,0,1:T(8,128)(2,1)}, u32[]{:S(2)}, u32[]{:S(2)}) %collective-permute-start.2) | collective-permute-done | bytes 9437216 | tf_op jit(solution)/shard_map/ppermute | solution.py:43
  332.6 7.8 %constant_dynamic-update-slice_fusion.7 = bf16[12288,2,1536]{2,0,1:T(8,128)(2,1)} fusion(bf16[1536,2,1536]{2,0,1:T(8,128)(2,1)} %collective-permute-done.2), kind=kLoop, calls=%fused_computation.71 | loop fusion | bytes 18874368
  340.5 7.9 %constant_dynamic-update-slice_fusion.6 = bf16[12288,2,1536]{2,0,1:T(8,128)(2,1)} fusion(bf16[12288,2,1536]{2,0,1:T(8,128)(2,1)} %constant_dynamic-update-slice_fusion.7, bf16[1536,2,1536]{2,0,1:T(8,128)(2,1)} %collective-permute-done.1), kind=kLoop, calls=%fused_computation.70 | loop fusion | bytes 18874368
  348.4 7.9 %constant_dynamic-update-slice_fusion.5 = bf16[12288,2,1536]{2,0,1:T(8,128)(2,1)} fusion(bf16[12288,2,1536]{2,0,1:T(8,128)(2,1)} %constant_dynamic-update-slice_fusion.6, bf16[1536,2,1536]{2,0,1:T(8,128)(2,1)} %copy-done.2), kind=kLoop, calls=%fused_computation.69 | loop fusion | bytes 18874368
  356.3 8.7 %constant_dynamic-update-slice_fusion.4 = bf16[12288,2,1536]{2,0,1:T(8,128)(2,1)} fusion(bf16[12288,2,1536]{2,0,1:T(8,128)(2,1)} %constant_dynamic-update-slice_fusion.5, bf16[1536,2,1536]{2,1,0:T(2,128)(2,1)} %param.11), kind=kLoop, calls=%fused_computation.68 | loop fusion | bytes 18874368
  365.0 7.8 %constant_dynamic-update-slice_fusion.3 = bf16[12288,2,1536]{2,0,1:T(8,128)(2,1)} fusion(bf16[12288,2,1536]{2,0,1:T(8,128)(2,1)} %constant_dynamic-update-slice_fusion.4, bf16[1536,2,1536]{2,0,1:T(8,128)(2,1)} %collective-permute-done.2), kind=kLoop, calls=%fused_computation.67 | loop fusion | bytes 18874368
  372.9 7.9 %constant_dynamic-update-slice_fusion.2 = bf16[12288,2,1536]{2,0,1:T(8,128)(2,1)} fusion(bf16[12288,2,1536]{2,0,1:T(8,128)(2,1)} %constant_dynamic-update-slice_fusion.3, bf16[1536,2,1536]{2,0,1:T(8,128)(2,1)} %collective-permute-done.1), kind=kLoop, calls=%fused_computation.66 | loop fusion | bytes 18874368
  380.8 7.8 %constant_dynamic-update-slice_fusion.1 = bf16[12288,2,1536]{2,0,1:T(8,128)(2,1)} fusion(bf16[12288,2,1536]{2,0,1:T(8,128)(2,1)} %constant_dynamic-update-slice_fusion.2, bf16[1536,2,1536]{2,0,1:T(8,128)(2,1)} %copy-done.2), kind=kLoop, calls=%fused_computation.65 | loop fusion | bytes 18874368
  388.6 8.8 %constant_dynamic-update-slice_fusion = bf16[12288,2,1536]{2,0,1:T(8,128)(2,1)} fusion(bf16[12288,2,1536]{2,0,1:T(8,128)(2,1)} %constant_dynamic-update-slice_fusion.1, bf16[1536,2,1536]{2,1,0:T(2,128)(2,1)} %param.11), kind=kLoop, calls=%fused_computation.64 | loop fusion | bytes 18874368 | tf_op jit(solution)/shard_map/jit(_roll_dynamic)/concatenate | solution.py:44
  397.4 10.6 %fusion.10 = bf16[256,1536]{1,0:T(8,128)(2,1)} fusion(bf16[256,6144]{1,0:T(8,128)(2,1)S(1)} %bitcast.99, bf16[12288,2,1536]{2,0,1:T(8,128)(2,1)} %constant_dynamic-update-slice_fusion, s32[]{:T(128)S(6)} %select_n.18), kind=kOutput, calls=%fused_computation.19 | convolution fusion | flops 4832624640 | bytes 22806532 | tf_op jit(solution)/shard_map/dot_general | solution.py:47
  408.0 2.4 reshape.95
  410.4 16.0 %fusion.8 = bf16[514,1536]{1,0:T(8,128)(2,1)S(1)} fusion(bf16[514,6144]{1,0:T(8,128)(2,1)} %reshape.81, bf16[12288,2,1536]{2,0,1:T(8,128)(2,1)} %constant_dynamic-update-slice_fusion, s32[]{:T(128)S(6)} %select_n.18, s32[]{:T(128)S(6)} %add.54), kind=kOutput, calls=%fused_computation.15 | convolution fusion | flops 9702214656 | bytes 26843144 | tf_op jit(solution)/shard_map/dot_general | solution.py:48
  426.4 2.4 reshape.82
  428.9 3.1 fusion.63
  433.5 2.9 copy.117
  437.7 87.9 %all-reduce.6.cloned.1.call-done = bf16[16,2,128,257]{2,1,3,0:T(2,128)(2,1)} async-done(((bf16[16,2,128,257]{2,1,3,0:T(2,128)(2,1)}), bf16[16,2,128,257]{2,1,3,0:T(2,128)(2,1)}) %all-reduce.6.cloned.1.call-update) | async-done | bytes 2105360
  525.6 1.4 constant_dynamic-slice_fusion
  533.8 16.0 %all-gather.2.cloned.1.call-done = bf16[4,8,128,257]{2,0,3,1:T(4,128)(2,1)} async-done(((bf16[4,2,128,257]{2,0,3,1:T(4,128)(2,1)}), bf16[4,8,128,257]{2,0,3,1:T(4,128)(2,1)}) %all-gather.2.cloned.1.call-update) | async-done | bytes 2105360 | tf_op jit(solution)/shard_map/all_gather | solution.py:71
  549.9 2.4 fusion.17
  553.2 1.5 fusion.24
  555.9 1.1 copy.125
  557.0 36.5 %all-reduce.4.cloned.1.call-done = bf16[1024,512]{0,1:T(8,128)(2,1)} async-done(((bf16[1024,512]{0,1:T(8,128)(2,1)}), bf16[1024,512]{0,1:T(8,128)(2,1)}) %all-reduce.4.cloned.1.call-update) | async-done | bytes 1048592 | tf_op jit(solution)/shard_map/psum | solution.py:124
  593.5 2.6 copy.126
  (57 shorter events, 11.5 us)
Async XLA Ops:
  6.5 519.1 %all-reduce.6.cloned.1.call-start = ((), (), s32[]{:S(2)}) async-start(), calls=%async_computation.2 | async-start | bytes 4210688
  15.3 105.0 %collective-permute-start = (bf16[1536,2,1536]{2,0,1:T(8,128)(2,1)}, bf16[1536,2,1536]{2,0,1:T(8,128)(2,1)S(1)}, u32[]{:S(2)}, u32[]{:S(2)}) collective-permute-start(bf16[1536,2,1536]{2,0,1:T(8,128)(2,1)} %copy.110), channel_id=1, source_target_pairs={{0,1},{1,2},{2,3},{3,0},{4,5},{5,6},{6,7},{7,4},{8,9},{9,10},{10,1... | collective-permute-start | bytes 28311560 | tf_op jit(solution)/shard_map/ppermute | solution.py:43
  120.3 3.7 copy-start.2
  124.0 104.2 %collective-permute-start.1 = (bf16[1536,2,1536]{2,0,1:T(8,128)(2,1)S(1)}, bf16[1536,2,1536]{2,0,1:T(8,128)(2,1)}, u32[]{:S(2)}, u32[]{:S(2)}) collective-permute-start(bf16[1536,2,1536]{2,0,1:T(8,128)(2,1)S(1)} %collective-permute-done), channel_id=1, source_target_pairs={{0,1},{1,2},{2,3},{3,0},{4,5},{5,6},{6,7},{7,4},{8,9},{9,10},{10,1... | collective-permute-start | bytes 28311560 | tf_op jit(solution)/shard_map/ppermute | solution.py:43
  228.2 104.4 %collective-permute-start.2 = (bf16[1536,2,1536]{2,0,1:T(8,128)(2,1)}, bf16[1536,2,1536]{2,0,1:T(8,128)(2,1)}, u32[]{:S(2)}, u32[]{:S(2)}) collective-permute-start(bf16[1536,2,1536]{2,0,1:T(8,128)(2,1)} %collective-permute-done.1), channel_id=1, source_target_pairs={{0,1},{1,2},{2,3},{3,0},{4,5},{5,6},{6,7},{7,4},{8,9},{9,10},{10,1... | collective-permute-start | bytes 28311560 | tf_op jit(solution)/shard_map/ppermute | solution.py:43
  228.2 6.3 %copy-start = (bf16[2,257,6144]{2,0,1:T(2,128)(2,1)S(1)}, bf16[2,257,6144]{2,0,1:T(2,128)(2,1)}, u32[]{:S(2)}) copy-start(bf16[2,257,6144]{2,0,1:T(2,128)(2,1)} %param.9) | copy-start | bytes 18948100
  234.5 3.5 copy-start.6
  242.3 2.7 copy-start.1
  388.6 8.8 %slice-start = ((bf16[2,257,6144]{2,1,0:T(8,128)(2,1)}), bf16[2,128,6144]{2,1,0:T(8,128)(2,1)S(1)}, s32[]{:S(2)}) async-start(bf16[2,257,6144]{2,1,0:T(8,128)(2,1)} %copy-done.1), calls=%async_computation.3 | async-start | bytes 6291456 | tf_op jit(solution)/shard_map/slice | solution.py:39
  432.0 0.7 copy-start.7
  433.4 3.0 copy-start.11
  436.4 91.7 %copy-start.5 = (bf16[1024,512]{1,0:T(8,128)(2,1)S(1)}, bf16[1024,512]{1,0:T(8,128)(2,1)}, u32[]{:S(2)}) copy-start(bf16[1024,512]{1,0:T(8,128)(2,1)} %param.17) | copy-start | bytes 3145732
  436.4 113.4 %all-gather.2.cloned.1.call-start = ((), (), s32[]{:S(2)}) async-start(), calls=%async_computation | async-start | bytes 2631680 | tf_op jit(solution)/shard_map/all_gather | solution.py:71
  437.7 91.2 %copy-start.3 = (bf16[2,257,1024]{2,0,1:T(2,128)(2,1)S(1)}, bf16[2,257,1024]{2,0,1:T(2,128)(2,1)}, u32[]{:S(2)}) copy-start(bf16[2,257,1024]{2,0,1:T(2,128)(2,1)} %param.14) | copy-start | bytes 3158020
  528.1 65.4 %all-reduce.4.cloned.1.call-start = ((), (), s32[]{:S(2)}) async-start(), calls=%async_computation.1 | async-start | bytes 2097152 | tf_op jit(solution)/shard_map/psum | solution.py:124
  528.9 0.9 copy-start.8
  528.9 0.9 copy-start.9
  530.3 1.0 copy-start.4
  532.6 17.3 %copy-start.10 = (s32[2]{0:T(128)S(1)}, s32[2]{0:T(128)}, u32[]{:S(2)}) copy-start(s32[2]{0:T(128)} %param.13) | copy-start | bytes 28
Sparse Core Ops, SparseCore 0:
  436.5 89.0 all-reduce.5
  528.2 21.6 all-gather.1
  557.1 36.2 all-reduce.3
